TPU v7x, 32 devices: a whole 2x2x4 slice. The times are simulated.
32 devices in a mesh: grp: 2 (over y), seq: 4 (over z), head: 4 (over x, core).
Axes of the slice: x: 2, y: 2, z: 4, core: 2. Of those that a mesh axis runs over, the one named last changes fastest.
Arguments:
- queries: bfloat16 [5120, 8192], P(('grp', 'seq'), 'head'), parts along dimension 0, may hold values from -30 to 30, as said below
- keys: bfloat16 [5120, 8192], P(('grp', 'seq'), 'head'), parts along dimension 0, may hold values from -6 to 6
- values: bfloat16 [5120, 8192], P(('grp', 'seq'), 'head'), parts along dimension 0, may hold values from -24 to 24, as said below
- gain: bfloat16 [8192], P('head'), may hold values from 0.25 to 1.75
Outputs:
- output: bfloat16 [5120, 8192], P(('grp', 'seq'), 'head'), parts along dimension 0
There are 2 independent parts, one for each index of `grp`. A program takes and returns all parts, laid end to end along the dimension named above; an argument that names none is the same for every part. Nothing has to cross between parts.
Inputs may be any that keep to these rules, and one draw needn't show every extreme that they name: `queries`: query rows of various sizes. `values`: value features and rows of various sizes.
All inputs are finite; a program needn't handle non-finite values.
Results may differ from a plain program's by a relative error of at most 0.0051.
Values sent between devices are 32-bit elements; how exact they have to be, the bound alone decides.
No kernel may reach another device: no remote copies, remote signals or barrier semaphores. Data moves between devices by JAX's collectives and lax.ppermute only.
A program may use at most 64 MiB of HBM per device.

v0:
```python
import jax
import jax.numpy as jnp
from jax import lax
from jax.sharding import PartitionSpec as P

HEADS = 64
HEAD_DIM = 128


def body(queries, keys, values, gain):
    tokens_here = queries.shape[0]
    heads_here = queries.shape[1] // HEAD_DIM
    queries_split = queries.reshape(tokens_here, heads_here, HEAD_DIM)
    keys_split = keys.reshape(tokens_here, heads_here, HEAD_DIM)
    values_split = values.reshape(tokens_here, heads_here, HEAD_DIM)
    local_state = jnp.einsum(
        "thd,the->hde", keys_split, values_split, preferred_element_type=jnp.float32
    )
    my_index = lax.axis_index("seq")
    piece = lax.all_gather(local_state[None], "seq", axis=0, tiled=True)
    owners = jnp.arange(piece.shape[0], dtype=jnp.int32)
    weights = (owners < my_index).astype(jnp.float32)
    prefix = jnp.sum(piece * weights[:, None, None, None], axis=0)
    positions = jnp.arange(tokens_here)
    causal = positions[:, None] >= positions[None, :]
    scores = jnp.einsum(
        "thd,shd->hts", queries_split, keys_split, preferred_element_type=jnp.float32
    )
    scores = jnp.where(causal[None], scores, jnp.float32(0.0)).astype(jnp.bfloat16)
    intra_term = jnp.einsum(
        "hts,she->the", scores, values_split, preferred_element_type=jnp.float32
    )
    prefix_low = prefix.astype(jnp.bfloat16)
    inter_term = jnp.einsum(
        "thd,hde->the", queries_split, prefix_low, preferred_element_type=jnp.float32
    )
    mixed = (intra_term + inter_term).reshape(tokens_here, heads_here * HEAD_DIM)
    partial_squares = jnp.sum(mixed * mixed, axis=1)
    total_squares = lax.psum(partial_squares, "head")
    factor = lax.rsqrt(total_squares / (HEADS * HEAD_DIM) + 1e-06)
    return (mixed * factor[:, None] * gain.astype(jnp.float32)[None, :]).astype(jnp.bfloat16)


def solution(mesh):
    placed = (
        P(("grp", "seq"), "head"),
        P(("grp", "seq"), "head"),
        P(("grp", "seq"), "head"),
        P("head"),
    )
    return jax.shard_map(
        body, mesh=mesh, in_specs=placed, out_specs=P(("grp", "seq"), "head"), check_vma=False
    )
```

profile of v0, /device:TPU:0, one launch (start us, length us, event | category | flops | bytes accessed | tf_op | source)
XLA Modules:
  0.0 132.1 jit_solution(14653907628350191327)
XLA Ops:
  6.5 0.0 copy-start
  6.5 0.0 all-gather.3.cloned.1.call-start
  6.5 4.5 %copy.17 = bf16[640,2048]{0,1:T(8,128)(2,1)} copy(bf16[640,2048]{1,0:T(8,128)(2,1)} %param.5) | data formatting | bytes 5242880 | tf_op jit(solution)/shard_map/reshape | solution.py:14
  11.1 0.0 copy-start.1
  11.1 4.4 %fusion.2 = f32[16,128,128]{2,1,0:T(8,128)} fusion(bf16[640,16,128]{0,2,1:T(8,128)(2,1)} %bitcast.43, bf16[640,2048]{1,0:T(8,128)(2,1)} %param.6), kind=kOutput, calls=%fused_computation.7 | convolution fusion | flops 335544320 | bytes 6291456 | tf_op jit(solution)/shard_map/thd,the->hde/dot_general | solution.py:16
  15.4 0.0 all-gather.3.cloned.1.call-update
  15.5 0.0 copy-done.1
  15.5 0.1 iota_compare_fusion
  15.6 0.0 copy-done
  15.6 10.9 %fusion = f32[16,640,128]{1,2,0:T(8,128)} fusion(bf16[640,16,128]{0,2,1:T(8,128)(2,1)} %bitcast.44, pred[640,640]{1,0:T(8,128)(4,1)S(1)} %iota_compare_fusion, bf16[640,2048]{1,0:T(8,128)(2,1)} %param.6, bf16[640,2048]{1,0:T(8,128)(2,1)S(1)} %copy-done), kind=kOutput, calls=%fused_computation.5 | convolution fusion | flops 3368550400 | bytes 13516800 | tf_op jit(solution)/shard_map/hts,she->the/dot_general | solution.py:30
  26.5 72.6 %all-gather.3.cloned.1.call-done = f32[64,128,128]{2,1,0:T(8,128)} async-done(((f32[16,128,128]{2,1,0:T(8,128)}), f32[64,128,128]{2,1,0:T(8,128)}) %all-gather.3.cloned.1.call-update) | async-done | bytes 4194320 | tf_op jit(solution)/shard_map/all_gather | solution.py:20
  99.1 2.7 %multiply_reduce_fusion.1 = bf16[16,128,128]{2,1,0:T(8,128)(2,1)S(1)} fusion(f32[4,16,128,128]{3,2,1,0:T(8,128)} %bitcast.42, f32[4]{0:T(128)S(1)} %compare_convert_fusion), kind=kLoop, calls=%fused_computation.4 | loop fusion | flops 1835008 | bytes 4718608 | tf_op jit(solution)/shard_map/reduce_sum | solution.py:23
  101.8 6.0 %multiply_reduce_fusion = (f32[640]{0:T(1024)S(1)}, f32[640,16,128]{0,2,1:T(8,128)}) fusion(bf16[16,128,128]{2,1,0:T(8,128)(2,1)S(1)} %multiply_reduce_fusion.1, f32[16,640,128]{1,2,0:T(8,128)} %fusion, bf16[640,2048]{1,0:T(8,128)(2,1)S(1)} %copy-done), kind=kOutput, calls=%fused_computation.3 | convolution fusion | flops 339475840 | bytes 13634048 | tf_op jit(solution)/shard_map/thd,hde->the/dot_general | solution.py:34
  107.8 6.0 %copy.15 = f32[640,2048]{1,0:T(8,128)} copy(f32[640,2048]{0,1:T(8,128)} %bitcast.41) | data formatting | bytes 10485760 | tf_op jit(solution)/shard_map/reshape | solution.py:37
  113.9 6.9 %psum.7 = f32[640]{0:T(1024)S(1)} all-reduce(f32[640]{0:T(1024)S(1)} %get-tuple-element.5), channel_id=1, replica_groups=mesh['grp'=2,'seq'=4,'head'=4] {'head'}, use_global_device_ids=true, to_apply=%region_2.3 | all-reduce | flops 640 | bytes 5120 | tf_op jit(solution)/shard_map/psum | solution.py:39
  120.7 4.5 %multiply_convert_fusion = bf16[640,2048]{1,0:T(8,128)(2,1)} fusion(f32[640,2048]{1,0:T(8,128)} %copy.15, f32[2048]{0:T(1024)S(1)} %convert_element_type.22, f32[640]{0:T(1024)S(1)} %add_rsqrt_fusion), kind=kLoop, calls=%fused_computation.2 | loop fusion | flops 3932160 | bytes 7875072 | tf_op jit(solution)/shard_map/convert_element_type | solution.py:41
  (3 shorter events, 0.0 us)
Async XLA Ops:
  6.5 9.1 %copy-start = (bf16[640,2048]{1,0:T(8,128)(2,1)S(1)}, bf16[640,2048]{1,0:T(8,128)(2,1)}, u32[]{:S(2)}) copy-start(bf16[640,2048]{1,0:T(8,128)(2,1)} %param.4) | copy-start | bytes 7864324
  6.5 92.5 %all-gather.3.cloned.1.call-start = ((), (), s32[]{:S(2)}) async-start(), calls=%async_computation | async-start | bytes 5242880 | tf_op jit(solution)/shard_map/all_gather | solution.py:20
  11.1 4.4 %copy-start.1 = (bf16[2048]{0:T(1024)(128)(2,1)S(1)}, bf16[2048]{0:T(1024)(128)(2,1)}, u32[]{:S(2)}) copy-start(bf16[2048]{0:T(1024)(128)(2,1)} %param.7) | copy-start | bytes 12292
Sparse Core Ops, SparseCore 0:
  15.6 83.4 all-gather.2
where the time goes:
time: 132 us
  waiting for transfers between devices  72.6 us (55%)
  matrix products  21.3 us (16%)
  between operations  13.4 us (10%)
  local copies, waits for them, and re-layouts  10.6 us (8%)
  other arithmetic  7.33 us (6%)
  blocking collectives  6.86 us (5%)
    all_gather x1, waiting for transfers between devices, body(): piece = lax.all_gather(local_state[None], 'seq', axis=0, tiled=True)  72.6 us
    dot_general x1, matrix products, body(): jnp.einsum('hts,she->the', scores, values_split, preferred_element_type=j...  10.9 us
    psum x1, blocking collectives, body(): total_squares = lax.psum(partial_squares, 'head')  6.86 us
    reshape x1, local copies, waits for them, and re-layouts, body(): (intra_term + inter_term).reshape(tokens_here, heads_here * HEAD_DIM)  6.05 us
    dot_general x1, matrix products, body(): jnp.einsum('thd,hde->the', queries_split, prefix_low, preferred_element_t...  6.03 us
    reshape x1, local copies, waits for them, and re-layouts, body(): keys_split = keys.reshape(tokens_here, heads_here, HEAD_DIM)  4.52 us
    convert_element_type x1, other arithmetic, body(): (mixed * factor[:, None] * gain.astype(jnp.float32)[None, :]).astype(jnp....  4.47 us
    dot_general x1, matrix products, body(): jnp.einsum('thd,the->hde', keys_split, values_split, preferred_element_ty...  4.37 us
  transfers between devices with their start and end apart: 1, of which 1 were waited for; matrix products, arithmetic and copies ran while one was open for 8% of the time, Pallas kernels for 0%

commit v1 on v0

--- a/solution.py
+++ b/solution.py
@@ -17,7 +17,14 @@
         "thd,the->hde", keys_split, values_split, preferred_element_type=jnp.float32
     )
     my_index = lax.axis_index("seq")
-    piece = lax.all_gather(local_state[None], "seq", axis=0, tiled=True)
+    own = local_state[None]
+    devices = lax.axis_size("seq")
+    moving, parts = (own, [own])
+    for _ in range(devices - 1):
+        moving = lax.ppermute(moving, "seq", [(i, (i + 1) % devices) for i in range(devices)])
+        parts.insert(0, moving)
+    flat = jnp.concatenate(parts, axis=0)
+    piece = jnp.roll(flat, (lax.axis_index("seq") + 1) * own.shape[0], axis=0)
     owners = jnp.arange(piece.shape[0], dtype=jnp.int32)
     weights = (owners < my_index).astype(jnp.float32)
     prefix = jnp.sum(piece * weights[:, None, None, None], axis=0)

time: 132 us -> 118 us (0.89)
  between operations: 13.4 us -> 0.17 us
  local copies, waits for them, and re-layouts: 10.6 us -> 19.9 us
  waiting for transfers between devices: 72.6 us -> 66.3 us
  matrix products: 21.3 us -> 17.8 us
  starting transfers between devices: 0.01 us -> 3.03 us
  other arithmetic: 7.33 us -> 5.15 us
    all_gather x1 -> x0, waiting for transfers between devices: 72.6 us -> none  [body(): piece = lax.all_gather(local_state[None], 'seq', axis=0, tiled=True)]
    ppermute x0 -> x3, waiting for transfers between devices: none -> 66.3 us  [body(): lax.ppermute(moving, 'seq', [(i, (i + 1) % devices) for i in range(device...]
    unnamed x4 -> x19, local copies, waits for them, and re-layouts: 0.01 us -> 9.22 us
    ppermute x0 -> x3, starting transfers between devices: none -> 3.03 us  [body(): lax.ppermute(moving, 'seq', [(i, (i + 1) % devices) for i in range(device...]
    dot_general x1, matrix products: 6.03 us -> 3.61 us  [body(): jnp.einsum('thd,hde->the', queries_split, prefix_low, preferred_element_t...]
    reduce_sum x1, other arithmetic: 2.71 us -> 0.54 us  [body(): prefix = jnp.sum(piece * weights[:, None, None, None], axis=0)]
  transfers between devices with their start and end apart: 1 -> 3, of which waited for: 1 -> 3; matrix products, arithmetic and copies ran while one was open for 8% -> 9% of each run, Pallas kernels for 0% -> 0%
where the time goes in v1:
time: 118 us
  waiting for transfers between devices  66.3 us (56%)
  local copies, waits for them, and re-layouts  19.9 us (17%)
  matrix products  17.8 us (15%)
  blocking collectives  5.63 us (5%)
  other arithmetic  5.15 us (4%)
  starting transfers between devices  3.03 us (3%)
    ppermute x3, waiting for transfers between devices, body(): lax.ppermute(moving, 'seq', [(i, (i + 1) % devices) for i in range(device...  66.3 us
    dot_general x1, matrix products, body(): jnp.einsum('hts,she->the', scores, values_split, preferred_element_type=j...  10.8 us
    unnamed x19, local copies, waits for them, and re-layouts  9.22 us
    reshape x1, local copies, waits for them, and re-layouts, body(): (intra_term + inter_term).reshape(tokens_here, heads_here * HEAD_DIM)  6.04 us
    psum x1, blocking collectives, body(): total_squares = lax.psum(partial_squares, 'head')  5.63 us
    reshape x1, local copies, waits for them, and re-layouts, body(): keys_split = keys.reshape(tokens_here, heads_here, HEAD_DIM)  4.54 us
    convert_element_type x1, other arithmetic, body(): (mixed * factor[:, None] * gain.astype(jnp.float32)[None, :]).astype(jnp....  4.47 us
    dot_general x1, matrix products, body(): jnp.einsum('thd,hde->the', queries_split, prefix_low, preferred_element_t...  3.61 us
  transfers between devices with their start and end apart: 3, of which 3 were waited for; matrix products, arithmetic and copies ran while one was open for 9% of the time, Pallas kernels for 0%

profile of v1, /device:TPU:0, one launch (start us, length us, event | category | flops | bytes accessed | tf_op | source)
XLA Modules:
  0.0 118.0 jit_solution(18232689133772952135)
XLA Ops:
  0.0 0.0 copy-start
  0.0 4.5 %copy.17 = bf16[640,2048]{0,1:T(8,128)(2,1)} copy(bf16[640,2048]{1,0:T(8,128)(2,1)} %param.5) | data formatting | bytes 5242880 | tf_op jit(solution)/shard_map/reshape | solution.py:14
  4.5 3.4 %fusion.16 = f32[1,16,128,128]{3,2,1,0:T(8,128)S(1)} fusion(bf16[640,16,128]{0,2,1:T(8,128)(2,1)} %bitcast.47, bf16[640,2048]{1,0:T(8,128)(2,1)} %param.6), kind=kOutput, calls=%fused_computation.17 | convolution fusion | flops 335544320 | bytes 6291456 | tf_op jit(solution)/shard_map/thd,the->hde/dot_general | solution.py:16
  7.9 0.0 copy-start.1
  7.9 1.0 copy-done.1
  8.9 3.0 %collective-permute-start = (f32[1,16,128,128]{3,2,1,0:T(8,128)S(1)}, f32[1,16,128,128]{3,2,1,0:T(8,128)}, u32[]{:S(2)}, u32[]{:S(2)}) collective-permute-start(f32[1,16,128,128]{3,2,1,0:T(8,128)S(1)} %fusion.16), channel_id=1, source_target_pairs={{0,4},{4,8},{8,12},{12,0},{1,5},{5,9},{9,13},{13,1},{2,6},{6,10},{... | collective-permute-start | bytes 3145736 | tf_op jit(solution)/shard_map/ppermute | solution.py:24
  12.0 25.3 %collective-permute-done = f32[1,16,128,128]{3,2,1,0:T(8,128)} collective-permute-done((f32[1,16,128,128]{3,2,1,0:T(8,128)S(1)}, f32[1,16,128,128]{3,2,1,0:T(8,128)}, u32[]{:S(2)}, u32[]{:S(2)}) %collective-permute-start) | collective-permute-done | bytes 1048608 | tf_op jit(solution)/shard_map/ppermute | solution.py:24
  37.2 0.0 collective-permute-start.1
  37.2 0.0 copy-done.3
  37.3 0.1 iota_compare_fusion
  37.4 26.3 %collective-permute-done.1 = f32[1,16,128,128]{3,2,1,0:T(8,128)} collective-permute-done((f32[1,16,128,128]{3,2,1,0:T(8,128)}, f32[1,16,128,128]{3,2,1,0:T(8,128)}, u32[]{:S(2)}, u32[]{:S(2)}) %collective-permute-start.1) | collective-permute-done | bytes 1048608 | tf_op jit(solution)/shard_map/ppermute | solution.py:24
  63.7 0.0 collective-permute-start.2
  63.7 0.0 copy-done
  63.7 10.8 %fusion = f32[16,640,128]{1,2,0:T(8,128)} fusion(bf16[640,16,128]{0,2,1:T(8,128)(2,1)} %bitcast.48, pred[640,640]{1,0:T(8,128)(4,1)S(1)} %iota_compare_fusion, bf16[640,2048]{1,0:T(8,128)(2,1)} %param.6, bf16[640,2048]{1,0:T(8,128)(2,1)S(1)} %copy-done), kind=kOutput, calls=%fused_computation.5 | convolution fusion | flops 3368550400 | bytes 13516800 | tf_op jit(solution)/shard_map/hts,she->the/dot_general | solution.py:37
  74.5 14.7 %collective-permute-done.2 = f32[1,16,128,128]{3,2,1,0:T(8,128)} collective-permute-done((f32[1,16,128,128]{3,2,1,0:T(8,128)}, f32[1,16,128,128]{3,2,1,0:T(8,128)}, u32[]{:S(2)}, u32[]{:S(2)}) %collective-permute-start.2) | collective-permute-done | bytes 1048608 | tf_op jit(solution)/shard_map/ppermute | solution.py:24
  89.2 1.3 %constant_dynamic-update-slice_fusion.7 = f32[8,16,128,128]{3,2,1,0:T(8,128)S(1)} fusion(f32[1,16,128,128]{3,2,1,0:T(8,128)} %collective-permute-done.2), kind=kLoop, calls=%fused_computation.26 | loop fusion | bytes 2097152
  90.6 1.3 %constant_dynamic-update-slice_fusion.6 = f32[8,16,128,128]{3,2,1,0:T(8,128)S(1)} fusion(f32[8,16,128,128]{3,2,1,0:T(8,128)S(1)} %constant_dynamic-update-slice_fusion.7, f32[1,16,128,128]{3,2,1,0:T(8,128)} %collective-permute-done.1), kind=kLoop, calls=%fused_computation.25 | loop fusion | bytes 2097152
  91.9 1.3 %constant_dynamic-update-slice_fusion.5 = f32[8,16,128,128]{3,2,1,0:T(8,128)S(1)} fusion(f32[8,16,128,128]{3,2,1,0:T(8,128)S(1)} %constant_dynamic-update-slice_fusion.6, f32[1,16,128,128]{3,2,1,0:T(8,128)} %collective-permute-done), kind=kLoop, calls=%fused_computation.24 | loop fusion | bytes 2097152
  93.2 0.0 copy-done.2
  93.2 0.0 slice-start
  93.2 0.1 constant_dynamic-update-slice_fusion.4
  93.3 1.5 %constant_dynamic-update-slice_fusion.3 = f32[8,16,128,128]{3,2,1,0:T(8,128)S(1)} fusion(f32[8,16,128,128]{3,2,1,0:T(8,128)S(1)} %constant_dynamic-update-slice_fusion.4, f32[1,16,128,128]{3,2,1,0:T(8,128)} %collective-permute-done.2), kind=kLoop, calls=%fused_computation.22 | loop fusion | bytes 2097152
  94.8 1.3 %constant_dynamic-update-slice_fusion.2 = f32[8,16,128,128]{3,2,1,0:T(8,128)S(1)} fusion(f32[8,16,128,128]{3,2,1,0:T(8,128)S(1)} %constant_dynamic-update-slice_fusion.3, f32[1,16,128,128]{3,2,1,0:T(8,128)} %collective-permute-done.1), kind=kLoop, calls=%fused_computation.21 | loop fusion | bytes 2097152
  96.1 0.0 slice-start.1
  96.1 1.4 %constant_dynamic-update-slice_fusion.1 = f32[8,16,128,128]{3,2,1,0:T(8,128)S(1)} fusion(f32[8,16,128,128]{3,2,1,0:T(8,128)S(1)} %constant_dynamic-update-slice_fusion.2, f32[1,16,128,128]{3,2,1,0:T(8,128)} %collective-permute-done), kind=kLoop, calls=%fused_computation.20 | loop fusion | bytes 2097152
  97.5 0.1 constant_dynamic-update-slice_fusion
  97.6 0.5 multiply_reduce_fusion.1
  98.2 0.0 slice-done
  98.2 3.6 %multiply_reduce_fusion = (f32[640]{0:T(1024)S(1)}, f32[640,16,128]{0,2,1:T(8,128)}) fusion(bf16[16,128,128]{2,1,0:T(8,128)(2,1)S(1)} %multiply_reduce_fusion.1, f32[16,640,128]{1,2,0:T(8,128)S(1)} %bitcast.46, bf16[640,2048]{1,0:T(8,128)(2,1)S(1)} %copy-done), kind=kOutput, calls=%fused_computation.3 | convolution fusion | flops 339475840 | bytes 13634048 | tf_op jit(solution)/shard_map/thd,hde->the/dot_general | solution.py:41
  101.8 6.0 %copy.15 = f32[640,2048]{1,0:T(8,128)} copy(f32[640,2048]{0,1:T(8,128)} %bitcast.44) | data formatting | bytes 10485760 | tf_op jit(solution)/shard_map/reshape | solution.py:44
  107.9 5.6 %psum.7 = f32[640]{0:T(1024)S(1)} all-reduce(f32[640]{0:T(1024)S(1)} %get-tuple-element.5), channel_id=1, replica_groups=mesh['grp'=2,'seq'=4,'head'=4] {'head'}, use_global_device_ids=true, to_apply=%region_2.3 | all-reduce | flops 640 | bytes 5120 | tf_op jit(solution)/shard_map/psum | solution.py:46
  113.5 4.5 %multiply_convert_fusion = bf16[640,2048]{1,0:T(8,128)(2,1)} fusion(f32[640,2048]{1,0:T(8,128)} %copy.15, f32[2048]{0:T(1024)S(1)} %convert_element_type.22, f32[640]{0:T(1024)S(1)} %add_rsqrt_fusion), kind=kLoop, calls=%fused_computation.2 | loop fusion | flops 3932160 | bytes 7875072 | tf_op jit(solution)/shard_map/convert_element_type | solution.py:48
  (7 shorter events, 0.0 us)
Async XLA Ops:
  0.0 63.7 %copy-start = (bf16[640,2048]{1,0:T(8,128)(2,1)S(1)}, bf16[640,2048]{1,0:T(8,128)(2,1)}, u32[]{:S(2)}) copy-start(bf16[640,2048]{1,0:T(8,128)(2,1)} %param.4) | copy-start | bytes 7864324
  0.0 37.2 %copy-start.3 = (bf16[2048]{0:T(1024)(128)(2,1)S(1)}, bf16[2048]{0:T(1024)(128)(2,1)}, u32[]{:S(2)}) copy-start(bf16[2048]{0:T(1024)(128)(2,1)} %param.7) | copy-start | bytes 12292
  7.9 1.0 copy-start.1
  8.9 28.3 %collective-permute-start = (f32[1,16,128,128]{3,2,1,0:T(8,128)S(1)}, f32[1,16,128,128]{3,2,1,0:T(8,128)}, u32[]{:S(2)}, u32[]{:S(2)}) collective-permute-start(f32[1,16,128,128]{3,2,1,0:T(8,128)S(1)} %fusion.16), channel_id=1, source_target_pairs={{0,4},{4,8},{8,12},{12,0},{1,5},{5,9},{9,13},{13,1},{2,6},{6,10},{... | collective-permute-start | bytes 3145736 | tf_op jit(solution)/shard_map/ppermute | solution.py:24
  37.2 26.5 %collective-permute-start.1 = (f32[1,16,128,128]{3,2,1,0:T(8,128)}, f32[1,16,128,128]{3,2,1,0:T(8,128)}, u32[]{:S(2)}, u32[]{:S(2)}) collective-permute-start(f32[1,16,128,128]{3,2,1,0:T(8,128)} %collective-permute-done), channel_id=1, source_target_pairs={{0,4},{4,8},{8,12},{12,0},{1,5},{5,9},{9,13},{13,1},{2,6},{6,10},{... | collective-permute-start | bytes 3145736 | tf_op jit(solution)/shard_map/ppermute | solution.py:24
  63.7 25.5 %collective-permute-start.2 = (f32[1,16,128,128]{3,2,1,0:T(8,128)}, f32[1,16,128,128]{3,2,1,0:T(8,128)}, u32[]{:S(2)}, u32[]{:S(2)}) collective-permute-start(f32[1,16,128,128]{3,2,1,0:T(8,128)} %collective-permute-done.1), channel_id=1, source_target_pairs={{0,4},{4,8},{8,12},{12,0},{1,5},{5,9},{9,13},{13,1},{2,6},{6,10},{... | collective-permute-start | bytes 3145736 | tf_op jit(solution)/shard_map/ppermute | solution.py:24
  74.5 18.7 %copy-start.2 = (f32[1,16,128,128]{3,2,1,0:T(8,128)S(1)}, f32[1,16,128,128]{3,2,1,0:T(8,128)}, u32[]{:S(2)}) copy-start(f32[1,16,128,128]{3,2,1,0:T(8,128)} %copy-done.1) | copy-start | bytes 3145732
  93.2 5.0 %slice-start = ((s8[5242880]{0:T(1024)(128)(4,1)}), s8[4194304]{0:T(1024)(128)(4,1)S(1)}, s32[]{:S(2)}) async-start(s8[5242880]{0:T(1024)(128)(4,1)} %bitcast.45), calls=%async_computation | async-start | bytes 8388608
  96.1 2.1 %slice-start.1 = ((s8[5242880]{0:T(1024)(128)(4,1)}), s8[1048576]{0:T(1024)(128)(4,1)S(1)}, s32[]{:S(2)}) async-start(s8[5242880]{0:T(1024)(128)(4,1)} %bitcast.45), calls=%async_computation.1 | async-start | bytes 2097152
